TPU v7x, 256 devices: a whole 4x4x8 slice. The times are simulated.
256 devices in a mesh: segment: 2 (over x_lo), seq: 16 (over y, x_hi, core), mp: 8 (over z).
Axes of the slice: x: 4 (x_hi: 2, x_lo: 2; x = x_hi * 2 + x_lo), y: 4, z: 8, core: 2. Of those that a mesh axis runs over, the one named last changes fastest.
Arguments:
- enc_states: bfloat16 [4096, 4096], P('seq', 'mp'), may hold values from -6 to 6
- dec_states: bfloat16 [4096, 4096], P('seq', 'mp'), may hold values from -21 to 21
- section_weights: bfloat16 [2, 4096, 2, 4096], P('segment', None, None, 'mp'), may hold values from -3 to 3
- group_lengths: int32 [32], P('seq'), may hold values from 1 to 128, 3072 in all
Outputs:
- mixed: bfloat16 [4096, 4096], P('seq', ('segment', 'mp'))
Inputs may be any that keep to these rules, and one draw needn't show every extreme that they name: Rows c * 128 to c * 128 + group_lengths[c] - 1 of the memory are real, the rest of block c is padding.
All inputs are finite; a program needn't handle non-finite values.
Results may differ from a plain program's by a relative error of at most 0.018.
Values may be sent and summed in bfloat16 or wider, within the bound.
A program may use at most 128 MiB of HBM per device.

v0:
```python
import math
import jax
import jax.numpy as jnp
from jax import lax
from jax.sharding import PartitionSpec as P

DH = 256
GROUP = 128


def from_behind(value, axis, steps):
    count = lax.axis_size(axis)
    leading, last = (max(0, -steps), min(count, count - steps))
    return lax.ppermute(value, axis, [(source, source + steps) for source in range(leading, last)])


def local(enc_states, dec_states, section_weights, group_lengths):
    encoder_side = lax.axis_index("segment") == 0
    local_weight = section_weights[0]
    width = local_weight.shape[0]
    columns = local_weight.shape[2]
    enc_rows = enc_states.shape[0]
    dec_rows = dec_states.shape[0]
    heads = columns // DH
    scale = DH ** (-0.5)
    start_sums = (
        jnp.zeros((enc_rows, 2 * columns), jnp.float32),
        jnp.zeros((dec_rows, columns), jnp.float32),
    )
    pieces = (
        lax.all_gather(enc_states, "mp", axis=1, tiled=True),
        lax.all_gather(dec_states, "mp", axis=1, tiled=True),
    )
    rows_in = pieces[0].shape[1]

    def encoder_work(state):
        update = jnp.dot(
            pieces[0],
            local_weight.reshape(rows_in, 2 * columns),
            preferred_element_type=jnp.float32,
        )
        return (update, state[1])

    def decoder_work(state):
        update = jnp.dot(pieces[1], local_weight[:, 0, :], preferred_element_type=jnp.float32)
        return (state[0], update)

    memory_sum, query_sum = lax.cond(encoder_side, encoder_work, decoder_work, start_sums)
    memory = memory_sum.astype(jnp.bfloat16)
    queries = query_sum.astype(jnp.bfloat16).reshape(dec_rows, heads, DH)
    received = from_behind(memory, "segment", 1)
    start_state = (
        jnp.full((dec_rows, heads), -1e30, jnp.float32),
        jnp.zeros((dec_rows, heads), jnp.float32),
        jnp.zeros((dec_rows, heads, DH), jnp.float32),
    )
    carry = start_state
    memory_piece = lax.all_gather(received, "seq", axis=0, tiled=True)
    length_piece = lax.all_gather(group_lengths, "seq", axis=0, tiled=True)
    amount = memory_piece.shape[0]
    span = math.gcd(amount, 1024)
    block_total = amount // span
    memory_blocks = memory_piece.reshape(block_total, span, 2 * columns)
    length_blocks = length_piece.reshape(block_total, span // GROUP)

    def one_block(state, item):
        best, total, accum = state
        block, lengths = item
        block_keys = block[:, :columns].reshape(span, heads, DH)
        block_values = block[:, columns:].reshape(span, heads, DH)
        scores = (
            jnp.einsum("qhd,khd->qhk", queries, block_keys, preferred_element_type=jnp.float32)
            * scale
        )
        valid = (jnp.arange(GROUP)[None, :] < lengths[:, None]).reshape(span)
        scores = jnp.where(valid[None, None, :], scores, -1e30)
        new_best = jnp.maximum(best, jnp.max(scores, axis=2))
        shrink = jnp.exp(best - new_best)
        weights = jnp.exp(scores - new_best[:, :, None]).astype(jnp.bfloat16)
        total = total * shrink + jnp.sum(weights, axis=2, dtype=jnp.float32)
        accum = accum * shrink[:, :, None] + jnp.einsum(
            "qhk,khd->qhd", weights, block_values, preferred_element_type=jnp.float32
        )
        return ((new_best, total, accum), None)

    carry, _ = lax.scan(one_block, carry, (memory_blocks, length_blocks))
    best, total, accum = carry
    attended = (accum / total[:, :, None]).astype(jnp.bfloat16).reshape(dec_rows, columns)

    def no_term(operand):
        return jnp.zeros((dec_rows, width), jnp.float32)

    def output_term(operand):
        projected = lax.dot_general(
            operand,
            local_weight[:, 1, :],
            (((1,), (1,)), ((), ())),
            preferred_element_type=jnp.float32,
        )
        offset = lax.axis_index("mp") * columns
        current = lax.dynamic_slice_in_dim(projected, offset, columns, 1)
        return lax.dynamic_update_slice_in_dim(
            projected, current + dec_states.astype(jnp.float32), offset, 1
        )

    term = lax.cond(encoder_side, no_term, output_term, attended)
    return lax.psum_scatter(
        term.astype(jnp.bfloat16), ("segment", "mp"), scatter_dimension=1, tiled=True
    )


def solution(mesh):
    in_specs = (P("seq", "mp"), P("seq", "mp"), P("segment", None, None, "mp"), P("seq"))
    out_specs = P("seq", ("segment", "mp"))
    return jax.shard_map(local, mesh=mesh, in_specs=in_specs, out_specs=out_specs, check_vma=False)
```

profile of v0, /device:TPU:8, one launch (start us, length us, event | category | flops | bytes accessed | tf_op | source)
XLA Modules:
  0.0 328.2 jit_solution(9274638926449847188)
XLA Ops:
  6.5 0.7 all-gather.6.cloned.1.call-update
  7.3 0.7 all-gather.4.cloned.1.call-update
  8.1 8.0 %copy.20 = bf16[1,4096,2,512]{3,1,2,0:T(8,128)(2,1)} copy(bf16[1,4096,2,512]{3,2,1,0:T(2,128)(2,1)} %param.12) | data formatting | bytes 16777216 | tf_op args[2]
  16.0 37.2 %all-gather.6.cloned.1.call-done = bf16[256,4096]{1,0:T(8,128)(2,1)} async-done(((bf16[256,512]{1,0:T(8,128)(2,1)}), bf16[256,4096]{1,0:T(8,128)(2,1)}) %all-gather.6.cloned.1.call-update) | async-done | bytes 2097168 | tf_op jit(solution)/shard_map/all_gather | solution.py:31
  53.2 41.5 %all-gather.4.cloned.1.call-done = bf16[256,4096]{1,0:T(8,128)(2,1)} async-done(((bf16[256,512]{1,0:T(8,128)(2,1)}), bf16[256,4096]{1,0:T(8,128)(2,1)}) %all-gather.4.cloned.1.call-update) | async-done | bytes 2097168 | tf_op jit(solution)/shard_map/all_gather | solution.py:32
  94.7 15.2 %conditional.2 = (bf16[256,1024]{1,0:T(8,128)(2,1)S(1)}, bf16[256,512]{1,0:T(8,128)(2,1)S(1)}) conditional(s32[]{:T(128)} %convert_element_type.25, (bf16[4096,2,512]{2,0,1:T(8,128)(2,1)}, bf16[256,4096]{1,0:T(8,128)(2,1)}) %tuple.67, (bf16[1,4096,2,512]{3,2,1,0:T(2,128)(2,1)}, bf16[256,4096]{1,0:T(8,128)(2,1)}) %tuple.24), branch_computations={%region_0.0_spmd, %region_1.0_spmd} | conditional | flops 2147483648 | bytes 36438064 | solution.py:48
  94.7 9.5 %copy.18 = bf16[512,8,2,512]{3,1,2,0:T(8,128)(2,1)} copy(bf16[512,8,2,512]{3,2,1,0:T(2,128)(2,1)} %bitcast.70) | data formatting | bytes 16777216 | tf_op jit(solution)/shard_map/cond
  104.2 5.7 %fusion.14 = bf16[256,1024]{1,0:T(8,128)(2,1)S(1)} fusion(bf16[256,4096]{1,0:T(8,128)(2,1)S(1)} %copy-done.4, bf16[4096,1024]{1,0:T(8,128)(2,1)} %bitcast.75), kind=kOutput, calls=%fused_computation.28 | convolution fusion | flops 2147483648 | bytes 11010048 | tf_op jit(solution)/shard_map/cond/branch_1_fun/dot_general | solution.py:37
  109.9 1.3 collective-permute-start
  111.2 7.7 %collective-permute-done = bf16[256,1024]{1,0:T(8,128)(2,1)S(1)} collective-permute-done((bf16[256,1024]{1,0:T(8,128)(2,1)S(1)}, bf16[256,1024]{1,0:T(8,128)(2,1)S(1)}, u32[]{:S(2)}, u32[]{:S(2)}) %collective-permute-start) | collective-permute-done | bytes 524320 | tf_op jit(solution)/shard_map/ppermute | solution.py:14
  119.0 0.8 copy-done.3
  119.9 0.6 dynamic-slice
  121.4 12.5 %all-reduce = s32[32]{0:T(128)S(1)} all-reduce(s32[32]{0:T(128)S(1)} %dynamic-update-slice), channel_id=1, replica_groups=mesh['segment'=2,'seq'=16,'mp'=8] {'seq'}, use_global_device_ids=true, to_apply=%add | all-reduce | flops 32 | bytes 256
  134.3 61.9 %all-gather.8.cloned.1.call-done = bf16[4096,1024]{1,0:T(8,128)(2,1)} async-done(((bf16[256,1024]{1,0:T(8,128)(2,1)}), bf16[4096,1024]{1,0:T(8,128)(2,1)}) %all-gather.8.cloned.1.call-update) | async-done | bytes 8388624 | tf_op jit(solution)/shard_map/all_gather | solution.py:58
  196.2 39.4 %while.15 = (s32[]{:T(128)}, f32[256,2]{0,1:T(2,128)S(1)}, f32[256,2]{0,1:T(2,128)S(1)}, f32[256,2,256]{0,2,1:T(8,128)}, s32[4,8]{1,0:T(4,128)S(1)}, /*index=5*/...) while((s32[]{:T(128)}, f32[256,2]{0,1:T(2,128)S(1)}, ...), condition=%wide.region_5.6_spmd.clone, body=%wide.region_2.5_spmd.clone.sunk | while | flops 544083456 | bytes 26513672 | solution.py:86
  196.3 3.1 constant_dynamic-slice_fusion.2
  199.4 2.9 copy.22
  202.5 1.0 bitcast_reduce_fusion.2
  203.5 0.5 convert_reduce_fusion.2
  204.0 0.5 copy-done.1
  204.5 0.7 fusion.39
  205.3 0.8 copy-done.2
  206.2 3.1 constant_dynamic-slice_fusion.2
  209.3 2.9 copy.22
  212.3 1.0 bitcast_reduce_fusion.2
  213.4 0.5 convert_reduce_fusion.2
  213.9 0.5 copy-done.1
  214.4 0.7 fusion.39
  215.1 0.8 copy-done.2
  216.0 3.1 constant_dynamic-slice_fusion.2
  219.1 2.9 copy.22
  222.2 1.0 bitcast_reduce_fusion.2
  223.2 0.5 convert_reduce_fusion.2
  223.7 0.5 copy-done.1
  224.2 0.7 fusion.39
  225.0 0.8 copy-done.2
  225.9 3.1 constant_dynamic-slice_fusion.2
  229.0 2.9 copy.22
  232.0 1.0 bitcast_reduce_fusion.2
  233.1 0.5 convert_reduce_fusion.2
  233.6 0.5 copy-done.1
  234.1 0.7 fusion.39
  234.8 0.8 copy-done.2
  235.7 1.1 divide_convert_fusion
  236.7 2.5 conditional.3
  236.8 2.5 broadcast.17
  239.2 3.8 %convert_element_type.29 = bf16[256,4096]{1,0:T(8,128)(2,1)} convert(f32[256,4096]{1,0:T(8,128)} %get-tuple-element.217) | non-fusion elementwise | flops 1048576 | bytes 6291456 | tf_op jit(solution)/shard_map/convert_element_type | solution.py:108
  243.1 78.6 %reduce-scatter.2.cloned.1.call-done = bf16[256,256]{1,0:T(8,128)(2,1)} async-done(((bf16[256,4096]{1,0:T(8,128)(2,1)}), bf16[256,256]{1,0:T(8,128)(2,1)}) %reduce-scatter.2.cloned.1.call-update) | async-done | bytes 131088 | tf_op jit(solution)/shard_map/reduce_scatter | solution.py:107
  (54 shorter events, 1.9 us)
Async XLA Ops:
  6.5 46.6 %all-gather.6.cloned.1.call-start = ((), (), s32[]{:S(2)}) async-start(), calls=%async_computation.2 | async-start | bytes 2359296 | tf_op jit(solution)/shard_map/all_gather | solution.py:31
  7.3 87.4 %all-gather.4.cloned.1.call-start = ((), (), s32[]{:S(2)}) async-start(), calls=%async_computation.1 | async-start | bytes 2359296 | tf_op jit(solution)/shard_map/all_gather | solution.py:32
  8.0 188.2 %all-gather.8.cloned.1.call-start = ((), (), s32[]{:S(2)}) async-start(), calls=%async_computation.3 | async-start | bytes 8912896 | tf_op jit(solution)/shard_map/all_gather | solution.py:58
  94.7 25.2 %copy-start.6 = (u32[256]{0:T(256)S(1)}, u32[256]{0:T(256)}, u32[]{:S(2)}) copy-start(u32[256]{0:T(256)} %constant.50) | copy-start | bytes 3076
  94.7 26.5 %copy-start.5 = (s32[2]{0:T(128)S(1)}, s32[2]{0:T(128)}, u32[]{:S(2)}) copy-start(s32[2]{0:T(128)} %param.13) | copy-start | bytes 28
  94.7 9.5 %copy-start.4 = (bf16[256,4096]{1,0:T(8,128)(2,1)S(1)}, bf16[256,4096]{1,0:T(8,128)(2,1)}, u32[]{:S(2)}) copy-start(bf16[256,4096]{1,0:T(8,128)(2,1)} %get-tuple-element.53) | copy-start | bytes 6291460 | tf_op jit(solution)/shard_map/cond
  109.9 9.1 %collective-permute-start = (bf16[256,1024]{1,0:T(8,128)(2,1)S(1)}, bf16[256,1024]{1,0:T(8,128)(2,1)S(1)}, u32[]{:S(2)}, u32[]{:S(2)}) collective-permute-start(bf16[256,1024]{1,0:T(8,128)(2,1)S(1)} %get-tuple-element.70), channel_id=1, source_target_pairs={{0,128},{1,129},{2,130},{3,131},{4,132},{5,133},{6,134},{7,135},{8... | collective-permute-start | bytes 1572872 | tf_op jit(solution)/shard_map/ppermute | solution.py:14
  119.0 0.8 copy-start.3
  119.8 201.9 %reduce-scatter.2.cloned.1.call-start = ((), (), s32[]{:S(2)}) async-start(), calls=%async_computation.4 | async-start | bytes 2228224 | tf_op jit(solution)/shard_map/reduce_scatter | solution.py:107
  203.5 1.0 copy-start.1
  205.3 0.8 copy-start.2
  213.3 1.0 copy-start.1
  215.1 0.8 copy-start.2
  223.2 1.0 copy-start.1
  225.0 0.8 copy-start.2
  233.0 1.0 copy-start.1
  234.8 0.8 copy-start.2
Sparse Core Ops, SparseCore 0:
  9.1 43.9 all-gather.5
  55.0 39.6 all-gather.3
  119.9 76.2 all-gather.7
  243.2 78.4 reduce-scatter.1
where the time goes:
time: 329 us; the launch traced here: 328 us
  waiting for transfers between devices  228 us (69%)
  local copies, waits for them, and re-layouts  51.7 us (16%)
  between operations  13.9 us (4%)
  matrix products  12.7 us (4%)
  blocking collectives  12.5 us (4%)
  other arithmetic  7.33 us (2%)
    reduce_scatter x1, waiting for transfers between devices, local(): lax.psum_scatter(term.astype(jnp.bfloat16), ('segment', 'mp'), scatter_di...  78.6 us
    all_gather x1, waiting for transfers between devices, local(): memory_piece = lax.all_gather(received, 'seq', axis=0, tiled=True)  61.9 us
    all_gather x1, waiting for transfers between devices, local(): lax.all_gather(dec_states, 'mp', axis=1, tiled=True)  41.5 us
    all_gather x1, waiting for transfers between devices, local(): lax.all_gather(enc_states, 'mp', axis=1, tiled=True)  37.2 us
    dynamic_slice x8, local copies, waits for them, and re-layouts, local(): carry, _ = lax.scan(one_block, carry, (memory_blocks, length_blocks))  23.8 us
    unnamed x1, blocking collectives  12.5 us
    unnamed x11, local copies, waits for them, and re-layouts  9.78 us
    cond x3, local copies, waits for them, and re-layouts  9.49 us
  transfers between devices with their start and end apart: 5, of which 5 were waited for; matrix products, arithmetic and copies ran while one was open for 3% of the time, Pallas kernels for 0%

commit v1 on v0

--- a/solution.py
+++ b/solution.py
@@ -3,9 +3,28 @@
 import jax.numpy as jnp
 from jax import lax
 from jax.sharding import PartitionSpec as P
+from jax.lax import axis_index, axis_size, ppermute
 
 DH = 256
 GROUP = 128
+
+
+def _recast_stops_all(z_in):
+    n_peers_all = axis_size("mp")
+    stack_in = []
+    for rr in range(n_peers_all):
+        stack_in.append((rr, (rr + 1) % n_peers_all))
+    seen = []
+    for rr in range(n_peers_all):
+        seen.append((rr, (rr - 1) % n_peers_all))
+    current_block, y1 = ([z_in], [z_in])
+    for _ in range(n_peers_all // 2):
+        current_block.append(ppermute(current_block[-1], "mp", stack_in))
+    for _ in range((n_peers_all - 1) // 2):
+        near = ppermute(y1[-1], "mp", seen)
+        y1.append(near)
+    front = jnp.concatenate([*current_block[::-1], *y1[1:]], axis=1)
+    return jnp.roll(front, shift=(axis_index("mp") - n_peers_all // 2) * z_in.shape[1], axis=1)
 
 
 def from_behind(value, axis, steps):
@@ -27,10 +46,7 @@
         jnp.zeros((enc_rows, 2 * columns), jnp.float32),
         jnp.zeros((dec_rows, columns), jnp.float32),
     )
-    pieces = (
-        lax.all_gather(enc_states, "mp", axis=1, tiled=True),
-        lax.all_gather(dec_states, "mp", axis=1, tiled=True),
-    )
+    pieces = (lax.all_gather(enc_states, "mp", axis=1, tiled=True), _recast_stops_all(dec_states))
     rows_in = pieces[0].shape[1]
 
     def encoder_work(state):

time: 329 us -> 302 us (0.918)
  waiting for transfers between devices: 228 us -> 186 us
  starting transfers between devices: 1.44 us -> 13.5 us
  matrix products: 12.7 us -> 18.9 us
    all_gather x1 -> x0, waiting for transfers between devices: 41.5 us -> none  [local(): lax.all_gather(dec_states, 'mp', axis=1, tiled=True)]
    all_gather x1, waiting for transfers between devices: 37.2 us -> 0.01 us  [local(): lax.all_gather(enc_states, 'mp', axis=1, tiled=True)]
    ppermute x0 -> x7, waiting for transfers between devices: none -> 33.5 us  [the longest x4 30.1 us: _recast_stops_all(): current_block.append(ppermute(current_block[-1], 'mp', stack_in))]
    ppermute x0 -> x7, starting transfers between devices: none -> 12 us  [the longest x3 10 us: _recast_stops_all(): near = ppermute(y1[-1], 'mp', seen)]
    dot_general x4, matrix products: 2.95 us -> 9.14 us  [one_block(): jnp.einsum('qhk,khd->qhd', weights, block_values, preferred_element_type=...]
    while x20 -> x4, local copies, waits for them, and re-layouts: 5.21 us -> 0.01 us
    all_gather x1, waiting for transfers between devices: 61.9 us -> 65.5 us  [local(): memory_piece = lax.all_gather(received, 'seq', axis=0, tiled=True)]
    unnamed x11 -> x30, local copies, waits for them, and re-layouts: 9.78 us -> 12.2 us
  transfers between devices with their start and end apart: 5 -> 11, of which waited for: 5 -> 9; matrix products, arithmetic and copies ran while one was open for 3% -> 3% of each run, Pallas kernels for 0% -> 0%
where the time goes in v1:
time: 302 us; the launch traced here: 301 us
  waiting for transfers between devices  186 us (62%)
  local copies, waits for them, and re-layouts  48.9 us (16%)
  matrix products  18.9 us (6%)
  between operations  14 us (5%)
  starting transfers between devices  13.5 us (4%)
  blocking collectives  12.4 us (4%)
  other arithmetic  7.32 us (2%)
    reduce_scatter x1, waiting for transfers between devices, local(): lax.psum_scatter(term.astype(jnp.bfloat16), ('segment', 'mp'), scatter_di...  78.6 us
    all_gather x1, waiting for transfers between devices, local(): memory_piece = lax.all_gather(received, 'seq', axis=0, tiled=True)  65.5 us
    ppermute x4, waiting for transfers between devices, _recast_stops_all(): current_block.append(ppermute(current_block[-1], 'mp', stack_in))  30.1 us
    dynamic_slice x8, local copies, waits for them, and re-layouts, local(): carry, _ = lax.scan(one_block, carry, (memory_blocks, length_blocks))  23.8 us
    unnamed x1, blocking collectives  12.4 us
    unnamed x30, local copies, waits for them, and re-layouts  12.2 us
    ppermute x3, starting transfers between devices, _recast_stops_all(): near = ppermute(y1[-1], 'mp', seen)  10 us
    cond x3, local copies, waits for them, and re-layouts  9.47 us
  transfers between devices with their start and end apart: 11, of which 9 were waited for; matrix products, arithmetic and copies ran while one was open for 3% of the time, Pallas kernels for 0%

profile of v1, /device:TPU:8, one launch (start us, length us, event | category | flops | bytes accessed | tf_op | source)
XLA Modules:
  0.0 301.3 jit_solution(9978434688633188064)
XLA Ops:
  6.5 0.7 all-gather.3.cloned.1.call-update
  7.3 2.0 collective-permute-start
  9.3 10.5 %collective-permute-done = bf16[256,512]{1,0:T(8,128)(2,1)S(1)} collective-permute-done((bf16[256,512]{1,0:T(8,128)(2,1)}, bf16[256,512]{1,0:T(8,128)(2,1)S(1)}, u32[]{:S(2)}, u32[]{:S(2)}) %collective-permute-start) | collective-permute-done | bytes 262176 | tf_op jit(solution)/shard_map/ppermute | solution.py:22
  19.8 3.2 %collective-permute-start.4 = (bf16[256,512]{1,0:T(8,128)(2,1)}, bf16[256,512]{1,0:T(8,128)(2,1)S(1)}, u32[]{:S(2)}, u32[]{:S(2)}) collective-permute-start(bf16[256,512]{1,0:T(8,128)(2,1)} %param.11), channel_id=1, source_target_pairs={{0,7},{1,0},{2,1},{3,2},{4,3},{5,4},{6,5},{7,6},{8,15},{9,8},{10,9... | collective-permute-start | bytes 786440 | tf_op jit(solution)/shard_map/ppermute | solution.py:24
  23.0 8.6 %collective-permute-done.1 = bf16[256,512]{1,0:T(8,128)(2,1)S(1)} collective-permute-done((bf16[256,512]{1,0:T(8,128)(2,1)S(1)}, bf16[256,512]{1,0:T(8,128)(2,1)S(1)}, u32[]{:S(2)}, u32[]{:S(2)}) %collective-permute-start.1) | collective-permute-done | bytes 262176 | tf_op jit(solution)/shard_map/ppermute | solution.py:22
  31.6 1.8 collective-permute-done.4
  33.4 3.6 %collective-permute-start.5 = (bf16[256,512]{1,0:T(8,128)(2,1)S(1)}, bf16[256,512]{1,0:T(8,128)(2,1)S(1)}, u32[]{:S(2)}, u32[]{:S(2)}) collective-permute-start(bf16[256,512]{1,0:T(8,128)(2,1)S(1)} %collective-permute-done.4), channel_id=1, source_target_pairs={{0,7},{1,0},{2,1},{3,2},{4,3},{5,4},{6,5},{7,6},{8,15},{9,8},{10,9... | collective-permute-start | bytes 786440 | tf_op jit(solution)/shard_map/ppermute | solution.py:24
  37.0 9.0 %collective-permute-done.2 = bf16[256,512]{1,0:T(8,128)(2,1)S(1)} collective-permute-done((bf16[256,512]{1,0:T(8,128)(2,1)S(1)}, bf16[256,512]{1,0:T(8,128)(2,1)S(1)}, u32[]{:S(2)}, u32[]{:S(2)}) %collective-permute-start.2) | collective-permute-done | bytes 262176 | tf_op jit(solution)/shard_map/ppermute | solution.py:22
  46.0 8.1 %copy.20 = bf16[1,4096,2,512]{3,1,2,0:T(8,128)(2,1)} copy(bf16[1,4096,2,512]{3,2,1,0:T(2,128)(2,1)} %param.12) | data formatting | bytes 16777216 | tf_op args[2]
  54.0 3.2 %collective-permute-start.6 = (bf16[256,512]{1,0:T(8,128)(2,1)S(1)}, bf16[256,512]{1,0:T(8,128)(2,1)S(1)}, u32[]{:S(2)}, u32[]{:S(2)}) collective-permute-start(bf16[256,512]{1,0:T(8,128)(2,1)S(1)} %collective-permute-done.5), channel_id=1, source_target_pairs={{0,7},{1,0},{2,1},{3,2},{4,3},{5,4},{6,5},{7,6},{8,15},{9,8},{10,9... | collective-permute-start | bytes 786440 | tf_op jit(solution)/shard_map/ppermute | solution.py:24
  57.3 2.1 collective-permute-done.3
  59.6 1.6 collective-permute-done.6
  61.5 1.9 copy-done.3
  63.4 15.2 %conditional.2 = (bf16[256,1024]{1,0:T(8,128)(2,1)S(1)}, bf16[256,512]{1,0:T(8,128)(2,1)S(1)}) conditional(s32[]{:T(128)} %convert_element_type.25, (s32[]{:T(128)}, s32[]{:T(128)}, bf16[256,8192]{1,0:T(8,128)(2,1)}, bf16[4096,2,512]{2,0,1:T(8,128)(2,1)}, s32[]{:T(128)}, /*index=5*/s32[]{:T(128)}) %tuple.83, ...), branch_computations={%region_0.1_spmd.clone, %region_1.2_spmd} | conditional | flops 2147483648 | bytes 36438064 | solution.py:64
  63.4 9.5 %copy.18 = bf16[512,8,2,512]{3,1,2,0:T(8,128)(2,1)} copy(bf16[512,8,2,512]{3,2,1,0:T(2,128)(2,1)} %bitcast.69) | data formatting | bytes 16777216 | tf_op jit(solution)/shard_map/cond
  72.9 5.7 %fusion.16 = bf16[256,1024]{1,0:T(8,128)(2,1)S(1)} fusion(bf16[256,4096]{1,0:T(8,128)(2,1)S(1)} %copy-done.4, bf16[4096,1024]{1,0:T(8,128)(2,1)} %bitcast.74), kind=kOutput, calls=%fused_computation.46 | convolution fusion | flops 2147483648 | bytes 11010048 | tf_op jit(solution)/shard_map/cond/branch_1_fun/dot_general | solution.py:53
  78.6 1.3 collective-permute-start.7
  79.9 7.9 %collective-permute-done.7 = bf16[256,1024]{1,0:T(8,128)(2,1)S(1)} collective-permute-done((bf16[256,1024]{1,0:T(8,128)(2,1)S(1)}, bf16[256,1024]{1,0:T(8,128)(2,1)S(1)}, u32[]{:S(2)}, u32[]{:S(2)}) %collective-permute-start.7) | collective-permute-done | bytes 524320 | tf_op jit(solution)/shard_map/ppermute | solution.py:33
  87.8 0.8 copy-done.2
  88.7 0.7 dynamic-slice
  90.3 12.4 %all-reduce = s32[32]{0:T(128)S(1)} all-reduce(s32[32]{0:T(128)S(1)} %dynamic-update-slice), channel_id=1, replica_groups=mesh['segment'=2,'seq'=16,'mp'=8] {'seq'}, use_global_device_ids=true, to_apply=%add | all-reduce | flops 32 | bytes 256
  103.1 65.5 %all-gather.5.cloned.1.call-done = bf16[4096,1024]{1,0:T(8,128)(2,1)} async-done(((bf16[256,1024]{1,0:T(8,128)(2,1)}), bf16[4096,1024]{1,0:T(8,128)(2,1)}) %all-gather.5.cloned.1.call-update) | async-done | bytes 8388624 | tf_op jit(solution)/shard_map/all_gather | solution.py:74
  168.6 40.3 %while.15 = (s32[]{:T(128)}, f32[256,2]{0,1:T(2,128)S(1)}, f32[256,2]{0,1:T(2,128)S(1)}, f32[256,2,256]{0,2,1:T(8,128)}, s32[4,8]{1,0:T(4,128)S(1)}, /*index=5*/...) while((s32[]{:T(128)}, f32[256,2]{0,1:T(2,128)S(1)}, ...), condition=%wide.region_5.6_spmd.clone, body=%wide.region_2.5_spmd.clone.sunk | while | flops 544083456 | bytes 22319312 | solution.py:102
  168.6 3.1 %constant_dynamic-slice_fusion.2 = bf16[1,1024,1024]{2,1,0:T(8,128)(2,1)} fusion(bf16[4,1024,1024]{2,1,0:T(8,128)(2,1)} %get-tuple-element.308, s32[]{:T(128)} %get-tuple-element.294), kind=kLoop, calls=%fused_computation.26.clone.1 | loop fusion | bytes 4194308 | tf_op jit(solution)/shard_map/while/body/jit(dynamic_index_in_dim)/dynamic_slice | solution.py:102
  171.7 2.9 copy.22
  174.8 1.0 bitcast_reduce_fusion.2
  175.8 0.5 convert_reduce_fusion.2
  176.3 1.5 fusion.40
  177.9 3.1 %constant_dynamic-slice_fusion.2 = bf16[1,1024,1024]{2,1,0:T(8,128)(2,1)} fusion(bf16[4,1024,1024]{2,1,0:T(8,128)(2,1)} %get-tuple-element.308, s32[]{:T(128)} %get-tuple-element.294), kind=kLoop, calls=%fused_computation.26.clone.1 | loop fusion | bytes 4194308 | tf_op jit(solution)/shard_map/while/body/jit(dynamic_index_in_dim)/dynamic_slice | solution.py:102
  181.0 2.9 copy.22
  184.1 1.0 bitcast_reduce_fusion.2
  185.1 0.5 convert_reduce_fusion.2
  185.6 2.5 fusion.40
  188.2 3.1 %constant_dynamic-slice_fusion.2 = bf16[1,1024,1024]{2,1,0:T(8,128)(2,1)} fusion(bf16[4,1024,1024]{2,1,0:T(8,128)(2,1)} %get-tuple-element.308, s32[]{:T(128)} %get-tuple-element.294), kind=kLoop, calls=%fused_computation.26.clone.1 | loop fusion | bytes 4194308 | tf_op jit(solution)/shard_map/while/body/jit(dynamic_index_in_dim)/dynamic_slice | solution.py:102
  191.3 2.9 copy.22
  194.4 1.0 bitcast_reduce_fusion.2
  195.4 0.5 convert_reduce_fusion.2
  195.9 2.5 fusion.40
  198.6 3.1 %constant_dynamic-slice_fusion.2 = bf16[1,1024,1024]{2,1,0:T(8,128)(2,1)} fusion(bf16[4,1024,1024]{2,1,0:T(8,128)(2,1)} %get-tuple-element.308, s32[]{:T(128)} %get-tuple-element.294), kind=kLoop, calls=%fused_computation.26.clone.1 | loop fusion | bytes 4194308 | tf_op jit(solution)/shard_map/while/body/jit(dynamic_index_in_dim)/dynamic_slice | solution.py:102
  201.7 2.9 copy.22
  204.7 1.0 bitcast_reduce_fusion.2
  205.7 0.5 convert_reduce_fusion.2
  206.3 2.5 fusion.40
  208.8 1.1 divide_convert_fusion
  209.9 2.5 conditional.3
  209.9 2.5 broadcast.18
  212.4 3.8 %convert_element_type.29 = bf16[256,4096]{1,0:T(8,128)(2,1)} convert(f32[256,4096]{1,0:T(8,128)} %get-tuple-element.312) | non-fusion elementwise | flops 1048576 | bytes 6291456 | tf_op jit(solution)/shard_map/convert_element_type | solution.py:124
  216.2 78.6 %reduce-scatter.2.cloned.1.call-done = bf16[256,256]{1,0:T(8,128)(2,1)} async-done(((bf16[256,4096]{1,0:T(8,128)(2,1)}), bf16[256,256]{1,0:T(8,128)(2,1)}) %reduce-scatter.2.cloned.1.call-update) | async-done | bytes 131088 | tf_op jit(solution)/shard_map/reduce_scatter | solution.py:123
  (69 shorter events, 2.3 us)
Async XLA Ops:
  6.5 56.9 %all-gather.3.cloned.1.call-start = ((), (), s32[]{:S(2)}) async-start(), calls=%async_computation.1 | async-start | bytes 2359296 | tf_op jit(solution)/shard_map/all_gather | solution.py:49
  7.3 161.3 %all-gather.5.cloned.1.call-start = ((), (), s32[]{:S(2)}) async-start(), calls=%async_computation.2 | async-start | bytes 8912896 | tf_op jit(solution)/shard_map/all_gather | solution.py:74
  7.3 12.5 %collective-permute-start = (bf16[256,512]{1,0:T(8,128)(2,1)}, bf16[256,512]{1,0:T(8,128)(2,1)S(1)}, u32[]{:S(2)}, u32[]{:S(2)}) collective-permute-start(bf16[256,512]{1,0:T(8,128)(2,1)} %param.11), channel_id=1, source_target_pairs={{0,1},{1,2},{2,3},{3,4},{4,5},{5,6},{6,7},{7,0},{8,9},{9,10},{10,1... | collective-permute-start | bytes 786440 | tf_op jit(solution)/shard_map/ppermute | solution.py:22
  19.8 11.9 %collective-permute-start.1 = (bf16[256,512]{1,0:T(8,128)(2,1)S(1)}, bf16[256,512]{1,0:T(8,128)(2,1)S(1)}, u32[]{:S(2)}, u32[]{:S(2)}) collective-permute-start(bf16[256,512]{1,0:T(8,128)(2,1)S(1)} %collective-permute-done), channel_id=1, source_target_pairs={{0,1},{1,2},{2,3},{3,4},{4,5},{5,6},{6,7},{7,0},{8,9},{9,10},{10,1... | collective-permute-start | bytes 786440 | tf_op jit(solution)/shard_map/ppermute | solution.py:22
  19.8 13.7 %collective-permute-start.4 = (bf16[256,512]{1,0:T(8,128)(2,1)}, bf16[256,512]{1,0:T(8,128)(2,1)S(1)}, u32[]{:S(2)}, u32[]{:S(2)}) collective-permute-start(bf16[256,512]{1,0:T(8,128)(2,1)} %param.11), channel_id=1, source_target_pairs={{0,7},{1,0},{2,1},{3,2},{4,3},{5,4},{6,5},{7,6},{8,15},{9,8},{10,9... | collective-permute-start | bytes 786440 | tf_op jit(solution)/shard_map/ppermute | solution.py:24
  31.6 14.3 %collective-permute-start.2 = (bf16[256,512]{1,0:T(8,128)(2,1)S(1)}, bf16[256,512]{1,0:T(8,128)(2,1)S(1)}, u32[]{:S(2)}, u32[]{:S(2)}) collective-permute-start(bf16[256,512]{1,0:T(8,128)(2,1)S(1)} %collective-permute-done.1), channel_id=1, source_target_pairs={{0,1},{1,2},{2,3},{3,4},{4,5},{5,6},{6,7},{7,0},{8,9},{9,10},{10,1... | collective-permute-start | bytes 786440 | tf_op jit(solution)/shard_map/ppermute | solution.py:22
  33.4 20.6 %collective-permute-start.5 = (bf16[256,512]{1,0:T(8,128)(2,1)S(1)}, bf16[256,512]{1,0:T(8,128)(2,1)S(1)}, u32[]{:S(2)}, u32[]{:S(2)}) collective-permute-start(bf16[256,512]{1,0:T(8,128)(2,1)S(1)} %collective-permute-done.4), channel_id=1, source_target_pairs={{0,7},{1,0},{2,1},{3,2},{4,3},{5,4},{6,5},{7,6},{8,15},{9,8},{10,9... | collective-permute-start | bytes 786440 | tf_op jit(solution)/shard_map/ppermute | solution.py:24
  46.0 13.4 %collective-permute-start.3 = (bf16[256,512]{1,0:T(8,128)(2,1)S(1)}, bf16[256,512]{1,0:T(8,128)(2,1)S(1)}, u32[]{:S(2)}, u32[]{:S(2)}) collective-permute-start(bf16[256,512]{1,0:T(8,128)(2,1)S(1)} %collective-permute-done.2), channel_id=1, source_target_pairs={{0,1},{1,2},{2,3},{3,4},{4,5},{5,6},{6,7},{7,0},{8,9},{9,10},{10,1... | collective-permute-start | bytes 786440 | tf_op jit(solution)/shard_map/ppermute | solution.py:22
  46.0 13.5 %copy-start = (bf16[256,512]{1,0:T(8,128)(2,1)S(1)}, bf16[256,512]{1,0:T(8,128)(2,1)}, u32[]{:S(2)}) copy-start(bf16[256,512]{1,0:T(8,128)(2,1)} %param.11) | copy-start | bytes 786436
  54.0 7.1 %collective-permute-start.6 = (bf16[256,512]{1,0:T(8,128)(2,1)S(1)}, bf16[256,512]{1,0:T(8,128)(2,1)S(1)}, u32[]{:S(2)}, u32[]{:S(2)}) collective-permute-start(bf16[256,512]{1,0:T(8,128)(2,1)S(1)} %collective-permute-done.5), channel_id=1, source_target_pairs={{0,7},{1,0},{2,1},{3,2},{4,3},{5,4},{6,5},{7,6},{8,15},{9,8},{10,9... | collective-permute-start | bytes 786440 | tf_op jit(solution)/shard_map/ppermute | solution.py:24
  61.4 1.9 copy-start.3
  63.4 25.3 %copy-start.6 = (u32[256]{0:T(256)S(1)}, u32[256]{0:T(256)}, u32[]{:S(2)}) copy-start(u32[256]{0:T(256)} %constant.94) | copy-start | bytes 3076
  63.4 26.7 %copy-start.5 = (s32[2]{0:T(128)S(1)}, s32[2]{0:T(128)}, u32[]{:S(2)}) copy-start(s32[2]{0:T(128)} %param.13) | copy-start | bytes 28
  63.4 9.5 %copy-start.4 = (bf16[256,4096]{1,0:T(8,128)(2,1)S(1)}, bf16[256,4096]{1,0:T(8,128)(2,1)}, u32[]{:S(2)}) copy-start(bf16[256,4096]{1,0:T(8,128)(2,1)} %get-tuple-element.128) | copy-start | bytes 6291460 | tf_op jit(solution)/shard_map/cond
  78.6 9.2 %collective-permute-start.7 = (bf16[256,1024]{1,0:T(8,128)(2,1)S(1)}, bf16[256,1024]{1,0:T(8,128)(2,1)S(1)}, u32[]{:S(2)}, u32[]{:S(2)}) collective-permute-start(bf16[256,1024]{1,0:T(8,128)(2,1)S(1)} %get-tuple-element.145), channel_id=1, source_target_pairs={{0,128},{1,129},{2,130},{3,131},{4,132},{5,133},{6,134},{7,135},{8... | collective-permute-start | bytes 1572872 | tf_op jit(solution)/shard_map/ppermute | solution.py:33
  87.8 0.8 copy-start.2
  88.6 206.2 %reduce-scatter.2.cloned.1.call-start = ((), (), s32[]{:S(2)}) async-start(), calls=%async_computation.3 | async-start | bytes 2228224 | tf_op jit(solution)/shard_map/reduce_scatter | solution.py:123
Sparse Core Ops, SparseCore 0:
  9.1 50.7 all-gather.2
  88.8 79.7 all-gather.4
  216.3 78.4 reduce-scatter.1
